TPU v7x, 32 devices: a whole 2x2x4 slice. The times are simulated.
32 devices in a mesh: span: 16 (over z, y, x), wall: 2 (over core).
Axes of the slice: x: 2, y: 2, z: 4, core: 2. Of those that a mesh axis runs over, the one named last changes fastest.
Arguments:
- velocity: bfloat16 [64, 3, 8, 128, 256], P(None, None, None, 'span', 'wall'), may hold values from -1080 to 1080, as said below
- wall_metric: float32 [256], P('wall'), may hold values from 0.5 to 2
Outputs:
- modes: bfloat16 [64, 3, 2, 128, 256], P(None, None, None, 'span', 'wall')
- r_factor: float32 [64, 64], replicated
Inputs may be any that keep to these rules, and one draw needn't show every extreme that they name: velocity fields of order up to a few hundred.
All inputs are finite; a program needn't handle non-finite values.
Results may differ from a plain program's by a relative error of at most 0.0063.
Values may be sent and summed in bfloat16 or wider, within the bound.
A program may use at most 64 MiB of HBM per device.

v0:
```python
import jax
import jax.numpy as jnp
from jax import lax
from jax.sharding import PartitionSpec as P


def padded_2(block, sides, width, periodic):
    for axis, dim in sides:
        count = lax.axis_size(axis)
        forward = [(i, i + 1) for i in range(count - 1)]
        if periodic:
            forward.append((count - 1, 0))
        backward = [(target, source) for source, target in forward]
        low = lax.ppermute(
            lax.slice_in_dim(block, block.shape[dim] - width, None, axis=dim), axis, forward
        )
        high = lax.ppermute(lax.slice_in_dim(block, 0, width, axis=dim), axis, backward)
        block = jnp.concatenate([low, block, high], axis=dim)
    return block


def stencil(padded, axis, length):

    def take(k):
        return lax.slice_in_dim(padded, 3 + k, 3 + k + length, axis=axis).astype(jnp.float32)

    return (45.0 * (take(1) - take(-1)) - 9.0 * (take(2) - take(-2)) + (take(3) - take(-3))) / 60.0


def factor_lower(gram):
    order = gram.shape[0]
    positions = jnp.arange(order, dtype=jnp.int32)

    def column(index, lower):
        at = jnp.asarray(index).astype(jnp.int32)
        above = lax.dynamic_slice_in_dim(gram, at, 1, 1)[:, 0]
        row_j = lax.dynamic_slice_in_dim(lower, at, 1, 0)[0]
        rest = above - jnp.sum(lower * row_j[None, :], axis=1)
        pivot = jnp.sqrt(lax.dynamic_slice_in_dim(rest, at, 1, 0)[0])
        keep = (positions >= at).astype(gram.dtype)
        pick = (positions == at).astype(gram.dtype)
        return lower + (keep * rest / pivot)[:, None] * pick[None, :]

    return lax.fori_loop(0, order, column, jnp.zeros_like(gram))


def invert_lower(lower):
    order = lower.shape[0]
    positions = jnp.arange(order, dtype=jnp.int32)

    def row_step(index, inverse):
        at = jnp.asarray(index).astype(jnp.int32)
        pick = (positions == at).astype(lower.dtype)
        row_l = lax.dynamic_slice_in_dim(lower, at, 1, 0)[0]
        pivot = lax.dynamic_slice_in_dim(row_l, at, 1, 0)[0]
        new_row = (pick - jnp.sum(row_l[:, None] * inverse, axis=0)) / pivot
        return inverse + pick[:, None] * new_row[None, :]

    return lax.fori_loop(0, order, row_step, jnp.zeros_like(lower))


def per_device(velocity, wall_metric):
    snaps = velocity.shape[0]
    planes = velocity.shape[2] - 6
    span_cells = velocity.shape[3]
    wall_cells = velocity.shape[4]
    inner = velocity[:, :, 3 : 3 + planes]
    span_padded = padded_2(inner, (("span", 3),), 3, True)
    wall_padded = padded_2(inner, (("wall", 4),), 3, False)
    du_dz = stencil(span_padded[:, 0], 2, span_cells)
    dv_dz = stencil(span_padded[:, 1], 2, span_cells)
    du_dy = wall_metric * stencil(wall_padded[:, 0], 3, wall_cells)
    dw_dy = wall_metric * stencil(wall_padded[:, 2], 3, wall_cells)
    dv_dx = stencil(velocity[:, 1], 1, planes)
    dw_dx = stencil(velocity[:, 2], 1, planes)
    vorticity = jnp.stack([dw_dy - dv_dz, du_dz - dw_dx, dv_dx - du_dy], axis=1).astype(
        jnp.bfloat16
    )
    flat = vorticity.reshape(snaps, -1)
    partial_gram = jnp.dot(flat, flat.T, preferred_element_type=jnp.float32)
    summed = lax.psum(partial_gram, ("span", "wall"))
    total_rows = (
        3 * planes * span_cells * lax.axis_size("span") * wall_cells * lax.axis_size("wall")
    )
    gram = summed / total_rows
    lower = factor_lower(gram)
    upper = lower.T
    r_inverse = invert_lower(lower).T.astype(jnp.bfloat16)
    modes = jnp.dot(r_inverse.T, flat, preferred_element_type=jnp.float32).astype(jnp.bfloat16)
    return (modes.reshape(vorticity.shape), upper)


def solution(mesh):
    in_specs = (P(None, None, None, "span", "wall"), P("wall"))
    out_specs = (P(None, None, None, "span", "wall"), P())
    return jax.shard_map(
        per_device, mesh=mesh, in_specs=in_specs, out_specs=out_specs, check_vma=False
    )
```

profile of v0, /device:TPU:0, one launch (start us, length us, event | category | flops | bytes accessed | tf_op | source)
XLA Modules:
  0.0 268.7 jit_solution(13451744703677940746)
XLA Ops:
  0.6 1.8 fusion.11
  2.4 0.8 copy.39
  3.2 2.9 %collective-permute-start.2 = (bf16[64,3,2,3,128]{4,0,3,2,1:T(8,128)(2,1)}, bf16[64,3,2,3,128]{4,0,3,2,1:T(8,128)(2,1)}, u32[]{:S(2)}, u32[]{:S(2)}) collective-permute-start(bf16[64,3,2,3,128]{4,0,3,2,1:T(8,128)(2,1)} %copy.39), channel_id=1, source_target_pairs={{0,2},{2,4},{4,6},{6,8},{8,10},{10,12},{12,14},{14,16},{16,18},{18... | collective-permute-start | bytes 884744 | tf_op jit(solution)/shard_map/ppermute | solution.py:14
  6.2 3.0 %fusion.13 = (bf16[64,3,2,8,3]{4,3,2,1,0:T(8,128)(2,1)}, bf16[64,3,2,8,3]{4,3,2,1,0:T(8,128)(2,1)}) fusion(bf16[64,3,8,8,128]{4,3,2,1,0:T(8,128)(2,1)} %param.6), kind=kLoop, calls=%fused_computation.43 | loop fusion | bytes 73728 | tf_op jit(solution)/shard_map/slice | solution.py:15
  9.1 2.4 copy.36
  11.5 2.1 collective-permute-start
  13.6 2.4 copy.38
  16.0 1.3 collective-permute-start.1
  17.3 0.8 copy.40
  18.1 4.3 %collective-permute-start.3 = (bf16[64,3,2,3,128]{4,0,3,2,1:T(8,128)(2,1)}, bf16[64,3,2,3,128]{4,0,3,2,1:T(8,128)(2,1)S(1)}, u32[]{:S(2)}, u32[]{:S(2)}) collective-permute-start(bf16[64,3,2,3,128]{4,0,3,2,1:T(8,128)(2,1)} %copy.40), channel_id=1, source_target_pairs={{2,0},{4,2},{6,4},{8,6},{10,8},{12,10},{14,12},{16,14},{18,16},{20... | collective-permute-start | bytes 884744 | tf_op jit(solution)/shard_map/ppermute | solution.py:17
  22.6 2.7 copy_bitcast_fusion
  25.3 1.3 copy.26
  26.5 1.2 copy.27
  27.8 1.0 constant_dynamic-update-slice_fusion.2
  31.4 0.7 subtract_bitcast_fusion
  34.0 40.6 %psum.7 = f32[64,64]{1,0:T(8,128)S(1)} all-reduce(f32[64,64]{1,0:T(8,128)S(1)} %convolution_bitcast_fusion), channel_id=1, replica_groups=mesh['span'=16,'wall'=2] {'span','wall'}, use_global_device_ids=true, to_apply=%region_0.0 | all-reduce | flops 4096 | bytes 32768 | tf_op jit(solution)/shard_map/psum | solution.py:81
  74.6 99.4 %while.33 = (s32[]{:T(128)}, f32[64,64]{1,0:T(8,128)S(1)}, f32[64,64]{0,1:T(8,128)S(1)}, s32[]{:T(128)}, s32[]{:T(128)}) while((s32[]{:T(128)}, f32[64,64]{1,0:T(8,128)S(1)}, f32[64,64]{0,1:T(8,128)S(1)}, s32[]{:T(128)}, s32[]{:T(128)}) %tuple.87), condition=%wide.region_3.0_spmd.clone.clone, body=%wide.region_1.0_spmd.clone.clone.sunk | while | flops 29059 | bytes 86889 | solution.py:44
  174.0 0.7 copy.34
  174.7 92.6 %while.32 = (s32[]{:T(128)}, f32[64,64]{1,0:T(8,128)S(1)}, f32[64,64]{1,0:T(8,128)S(1)}, s32[]{:T(128)}, s32[]{:T(128)}, /*index=5*/s32[]{:T(128)}) while((s32[]{:T(128)}, f32[64,64]{1,0:T(8,128)S(1)}, f32[64,64]{1,0:T(8,128)S(1)}, s32[]{:T(128)}, s32[]{:T(128)}, /*index=5*/s32[]{:T(128)}) %tuple.90), condition=%wide.region_6.0_spmd.clone, body=%wide.region_4.0_spmd.clone.sunk | while | flops 24900 | bytes 51580 | solution.py:59
  175.4 0.6 subtract_divide_fusion.2
  176.9 0.6 subtract_divide_fusion.2
  178.3 0.6 subtract_divide_fusion.2
  179.8 0.6 subtract_divide_fusion.2
  181.2 0.6 subtract_divide_fusion.2
  182.7 0.6 subtract_divide_fusion.2
  184.1 0.6 subtract_divide_fusion.2
  185.5 0.6 subtract_divide_fusion.2
  187.0 0.6 subtract_divide_fusion.2
  188.4 0.6 subtract_divide_fusion.2
  189.9 0.6 subtract_divide_fusion.2
  191.3 0.6 subtract_divide_fusion.2
  192.8 0.6 subtract_divide_fusion.2
  194.2 0.6 subtract_divide_fusion.2
  195.7 0.6 subtract_divide_fusion.2
  197.1 0.6 subtract_divide_fusion.2
  198.6 0.6 subtract_divide_fusion.2
  200.0 0.6 subtract_divide_fusion.2
  201.5 0.6 subtract_divide_fusion.2
  202.9 0.6 subtract_divide_fusion.2
  204.4 0.6 subtract_divide_fusion.2
  205.8 0.6 subtract_divide_fusion.2
  207.3 0.6 subtract_divide_fusion.2
  208.7 0.6 subtract_divide_fusion.2
  210.1 0.6 subtract_divide_fusion.2
  211.6 0.6 subtract_divide_fusion.2
  213.0 0.6 subtract_divide_fusion.2
  214.5 0.6 subtract_divide_fusion.2
  215.9 0.6 subtract_divide_fusion.2
  217.4 0.6 subtract_divide_fusion.2
  218.8 0.6 subtract_divide_fusion.2
  220.3 0.6 subtract_divide_fusion.2
  221.7 0.6 subtract_divide_fusion.2
  223.2 0.6 subtract_divide_fusion.2
  231.8 0.6 subtract_divide_fusion.2
  233.3 0.6 subtract_divide_fusion.2
  234.7 0.6 subtract_divide_fusion.2
  244.9 0.6 subtract_divide_fusion.2
  246.3 0.6 subtract_divide_fusion.2
  247.8 0.6 subtract_divide_fusion.2
  249.2 0.6 subtract_divide_fusion.2
  259.3 0.6 subtract_divide_fusion.2
  260.8 0.6 subtract_divide_fusion.2
  262.2 0.6 subtract_divide_fusion.2
  267.7 1.0 copy.44
  (882 shorter events, 120.2 us)
Async XLA Ops:
  3.2 24.5 %collective-permute-start.2 = (bf16[64,3,2,3,128]{4,0,3,2,1:T(8,128)(2,1)}, bf16[64,3,2,3,128]{4,0,3,2,1:T(8,128)(2,1)}, u32[]{:S(2)}, u32[]{:S(2)}) collective-permute-start(bf16[64,3,2,3,128]{4,0,3,2,1:T(8,128)(2,1)} %copy.39), channel_id=1, source_target_pairs={{0,2},{2,4},{4,6},{6,8},{8,10},{10,12},{12,14},{14,16},{16,18},{18... | collective-permute-start | bytes 884744 | tf_op jit(solution)/shard_map/ppermute | solution.py:14
  6.2 16.2 %copy-start = (bf16[64,3,8,8,128]{4,3,2,1,0:T(8,128)(2,1)S(1)}, bf16[64,3,8,8,128]{4,3,2,1,0:T(8,128)(2,1)}, u32[]{:S(2)}) copy-start(bf16[64,3,8,8,128]{4,3,2,1,0:T(8,128)(2,1)} %param.6) | copy-start | bytes 9437188
  11.5 13.7 %collective-permute-start = (bf16[64,3,2,8,3]{0,3,4,2,1:T(8,128)(2,1)}, bf16[64,3,2,8,3]{0,3,4,2,1:T(8,128)(2,1)}, u32[]{:S(2)}, u32[]{:S(2)}) collective-permute-start(bf16[64,3,2,8,3]{0,3,4,2,1:T(8,128)(2,1)} %copy.36), channel_id=1, source_target_pairs={{0,1},{2,3},{4,5},{6,7},{8,9},{10,11},{12,13},{14,15},{16,17},{18,... | collective-permute-start | bytes 55304 | tf_op jit(solution)/shard_map/ppermute | solution.py:14
  16.0 10.5 %collective-permute-start.1 = (bf16[64,3,2,8,3]{0,3,4,2,1:T(8,128)(2,1)}, bf16[64,3,2,8,3]{0,3,4,2,1:T(8,128)(2,1)}, u32[]{:S(2)}, u32[]{:S(2)}) collective-permute-start(bf16[64,3,2,8,3]{0,3,4,2,1:T(8,128)(2,1)} %copy.38), channel_id=1, source_target_pairs={{1,0},{3,2},{5,4},{7,6},{9,8},{11,10},{13,12},{15,14},{17,16},{19,... | collective-permute-start | bytes 55304 | tf_op jit(solution)/shard_map/ppermute | solution.py:17
  18.1 11.3 %collective-permute-start.3 = (bf16[64,3,2,3,128]{4,0,3,2,1:T(8,128)(2,1)}, bf16[64,3,2,3,128]{4,0,3,2,1:T(8,128)(2,1)S(1)}, u32[]{:S(2)}, u32[]{:S(2)}) collective-permute-start(bf16[64,3,2,3,128]{4,0,3,2,1:T(8,128)(2,1)} %copy.40), channel_id=1, source_target_pairs={{2,0},{4,2},{6,4},{8,6},{10,8},{12,10},{14,12},{16,14},{18,16},{20... | collective-permute-start | bytes 884744 | tf_op jit(solution)/shard_map/ppermute | solution.py:17
  22.5 2.7 %copy-start.3 = (f32[128]{0:T(128)S(1)}, f32[128]{0:T(128)}, u32[]{:S(2)}) copy-start(f32[128]{0:T(128)} %param.7) | copy-start | bytes 1540
  25.2 3.5 %slice-start = ((bf16[64,3,8,8,128]{4,3,2,1,0:T(8,128)(2,1)}), bf16[64,3,2,8,128]{4,3,2,1,0:T(8,128)(2,1)S(1)}, s32[]{:S(2)}) async-start(bf16[64,3,8,8,128]{4,3,2,1,0:T(8,128)(2,1)} %param.6), calls=%async_computation | async-start | bytes 1572864 | tf_op jit(solution)/shard_map/slice | solution.py:67
  30.1 1.2 copy-start.1
  31.3 1.2 copy-start.2
where the time goes:
time: 270 us; the launch traced here: 269 us
  local copies, waits for them, and re-layouts  98 us (36%)
  other arithmetic  69.6 us (26%)
  loops' own time  48.4 us (18%)
  blocking collectives  40.6 us (15%)
  starting transfers between devices  10.6 us (4%)
    another operation x1, loops' own time, factor_lower(): return lax.fori_loop(0, order, column, jnp.zeros_like(gram))  46.6 us
    div x64, other arithmetic, row_step(): new_row = (pick - jnp.sum(row_l[:, None] * inverse, axis=0)) / pivot  41.5 us
    psum x1, blocking collectives, per_device(): summed = lax.psum(partial_gram, ('span', 'wall'))  40.6 us
    dynamic_slice x64, local copies, waits for them, and re-layouts, column(): pivot = jnp.sqrt(lax.dynamic_slice_in_dim(rest, at, 1, 0)[0])  37.7 us
    dynamic_slice x64, local copies, waits for them, and re-layouts, row_step(): pivot = lax.dynamic_slice_in_dim(row_l, at, 1, 0)[0]  37.7 us
    unnamed x16, local copies, waits for them, and re-layouts  10.1 us
    reduce_sum x64, other arithmetic, column(): rest = above - jnp.sum(lower * row_j[None, :], axis=1)  6.84 us
    reduce_sum x64, other arithmetic, row_step(): new_row = (pick - jnp.sum(row_l[:, None] * inverse, axis=0)) / pivot  6.03 us
  transfers between devices with their start and end apart: 4, of which 1 were waited for; matrix products, arithmetic and copies ran while one was open for 6% of the time, Pallas kernels for 0%

commit v1 on v0

--- a/solution.py
+++ b/solution.py
@@ -2,6 +2,7 @@
 import jax.numpy as jnp
 from jax import lax
 from jax.sharding import PartitionSpec as P
+from jax.lax import psum
 
 
 def padded_2(block, sides, width, periodic):
@@ -78,7 +79,9 @@
     )
     flat = vorticity.reshape(snaps, -1)
     partial_gram = jnp.dot(flat, flat.T, preferred_element_type=jnp.float32)
-    summed = lax.psum(partial_gram, ("span", "wall"))
+    summed = partial_gram
+    for dd in ("wall", "span"):
+        summed = psum(summed, dd)
     total_rows = (
         3 * planes * span_cells * lax.axis_size("span") * wall_cells * lax.axis_size("wall")
     )

time: 270 us -> 311 us (1.15)
  blocking collectives: 40.6 us -> 81.3 us
    psum x1 -> x2, blocking collectives: 40.6 us -> 81.3 us  [per_device(): summed = psum(summed, dd)]
  transfers between devices with their start and end apart: 4 -> 4, of which waited for: 1 -> 1; matrix products, arithmetic and copies ran while one was open for 6% -> 5% of each run, Pallas kernels for 0% -> 0%
where the time goes in v1:
time: 311 us; the launch traced here: 310 us
  local copies, waits for them, and re-layouts  98 us (32%)
  blocking collectives  81.3 us (26%)
  other arithmetic  69.6 us (22%)
  loops' own time  48.4 us (16%)
  starting transfers between devices  10.5 us (3%)
    psum x2, blocking collectives, per_device(): summed = psum(summed, dd)  81.3 us
    another operation x1, loops' own time, factor_lower(): return lax.fori_loop(0, order, column, jnp.zeros_like(gram))  46.6 us
    div x64, other arithmetic, row_step(): new_row = (pick - jnp.sum(row_l[:, None] * inverse, axis=0)) / pivot  41.5 us
    dynamic_slice x64, local copies, waits for them, and re-layouts, column(): pivot = jnp.sqrt(lax.dynamic_slice_in_dim(rest, at, 1, 0)[0])  37.7 us
    dynamic_slice x64, local copies, waits for them, and re-layouts, row_step(): pivot = lax.dynamic_slice_in_dim(row_l, at, 1, 0)[0]  37.7 us
    unnamed x16, local copies, waits for them, and re-layouts  10.1 us
    reduce_sum x64, other arithmetic, column(): rest = above - jnp.sum(lower * row_j[None, :], axis=1)  6.87 us
  transfers between devices with their start and end apart: 4, of which 1 were waited for; matrix products, arithmetic and copies ran while one was open for 5% of the time, Pallas kernels for 0%

profile of v1, /device:TPU:0, one launch (start us, length us, event | category | flops | bytes accessed | tf_op | source)
XLA Modules:
  0.0 309.5 jit_solution(7354845102312188780)
XLA Ops:
  0.6 1.8 fusion.11
  2.4 0.8 copy.39
  3.2 2.9 collective-permute-start.2
  6.2 3.0 fusion.13
  9.1 2.4 copy.36
  11.6 2.1 collective-permute-start
  13.6 2.4 copy.38
  16.0 1.3 collective-permute-start.1
  17.3 0.8 copy.40
  18.1 4.3 %collective-permute-start.3 = (bf16[64,3,2,3,128]{4,0,3,2,1:T(8,128)(2,1)}, bf16[64,3,2,3,128]{4,0,3,2,1:T(8,128)(2,1)S(1)}, u32[]{:S(2)}, u32[]{:S(2)}) collective-permute-start(bf16[64,3,2,3,128]{4,0,3,2,1:T(8,128)(2,1)} %copy.40), channel_id=1, source_target_pairs={{2,0},{4,2},{6,4},{8,6},{10,8},{12,10},{14,12},{16,14},{18,16},{20... | collective-permute-start | bytes 884744 | tf_op jit(solution)/shard_map/ppermute | solution.py:18
  22.6 2.7 copy_bitcast_fusion
  25.3 1.3 copy.26
  26.6 1.2 copy.27
  27.8 1.0 constant_dynamic-update-slice_fusion.2
  31.4 0.7 subtract_bitcast_fusion
  34.0 4.6 %psum.14 = f32[64,64]{1,0:T(8,128)S(1)} all-reduce(f32[64,64]{1,0:T(8,128)S(1)} %convolution_bitcast_fusion), channel_id=1, replica_groups=mesh['span'=16,'wall'=2] {'wall'}, use_global_device_ids=true, to_apply=%region_0.0 | all-reduce | flops 4096 | bytes 32768 | tf_op jit(solution)/shard_map/psum | solution.py:84
  38.6 76.7 %psum.15 = f32[64,64]{1,0:T(8,128)S(1)} all-reduce(f32[64,64]{1,0:T(8,128)S(1)} %psum.14), channel_id=1, replica_groups=mesh['span'=16,'wall'=2] {'span'}, use_global_device_ids=true, to_apply=%region_1.0 | all-reduce | flops 4096 | bytes 32768 | tf_op jit(solution)/shard_map/psum | solution.py:84
  115.4 99.4 %while.33 = (s32[]{:T(128)}, f32[64,64]{1,0:T(8,128)S(1)}, f32[64,64]{0,1:T(8,128)S(1)}, s32[]{:T(128)}, s32[]{:T(128)}) while((s32[]{:T(128)}, f32[64,64]{1,0:T(8,128)S(1)}, f32[64,64]{0,1:T(8,128)S(1)}, s32[]{:T(128)}, s32[]{:T(128)}) %tuple.87), condition=%wide.region_4.0_spmd.clone.clone, body=%wide.region_2.0_spmd.clone.clone.sunk | while | flops 29059 | bytes 86889 | solution.py:45
  214.8 0.7 copy.34
  215.6 92.6 %while.32 = (s32[]{:T(128)}, f32[64,64]{1,0:T(8,128)S(1)}, f32[64,64]{1,0:T(8,128)S(1)}, s32[]{:T(128)}, s32[]{:T(128)}, /*index=5*/s32[]{:T(128)}) while((s32[]{:T(128)}, f32[64,64]{1,0:T(8,128)S(1)}, f32[64,64]{1,0:T(8,128)S(1)}, s32[]{:T(128)}, s32[]{:T(128)}, /*index=5*/s32[]{:T(128)}) %tuple.90), condition=%wide.region_7.0_spmd.clone, body=%wide.region_5.0_spmd.clone.sunk | while | flops 24900 | bytes 51580 | solution.py:60
  216.2 0.6 subtract_divide_fusion.2
  217.7 0.6 subtract_divide_fusion.2
  219.1 0.6 subtract_divide_fusion.2
  220.6 0.6 subtract_divide_fusion.2
  222.0 0.6 subtract_divide_fusion.2
  223.5 0.6 subtract_divide_fusion.2
  224.9 0.6 subtract_divide_fusion.2
  226.4 0.6 subtract_divide_fusion.2
  227.8 0.6 subtract_divide_fusion.2
  229.3 0.6 subtract_divide_fusion.2
  230.7 0.6 subtract_divide_fusion.2
  232.2 0.6 subtract_divide_fusion.2
  233.6 0.6 subtract_divide_fusion.2
  235.1 0.6 subtract_divide_fusion.2
  236.5 0.6 subtract_divide_fusion.2
  237.9 0.6 subtract_divide_fusion.2
  239.4 0.6 subtract_divide_fusion.2
  240.8 0.6 subtract_divide_fusion.2
  242.3 0.6 subtract_divide_fusion.2
  243.7 0.6 subtract_divide_fusion.2
  245.2 0.6 subtract_divide_fusion.2
  246.6 0.6 subtract_divide_fusion.2
  248.1 0.6 subtract_divide_fusion.2
  249.5 0.6 subtract_divide_fusion.2
  251.0 0.6 subtract_divide_fusion.2
  252.4 0.6 subtract_divide_fusion.2
  253.9 0.6 subtract_divide_fusion.2
  255.3 0.6 subtract_divide_fusion.2
  256.8 0.6 subtract_divide_fusion.2
  258.2 0.6 subtract_divide_fusion.2
  264.0 0.6 subtract_divide_fusion.2
  265.4 0.6 subtract_divide_fusion.2
  266.9 0.6 subtract_divide_fusion.2
  268.3 0.6 subtract_divide_fusion.2
  278.5 0.6 subtract_divide_fusion.2
  279.9 0.6 subtract_divide_fusion.2
  281.4 0.6 subtract_divide_fusion.2
  291.5 0.6 subtract_divide_fusion.2
  292.9 0.6 subtract_divide_fusion.2
  294.4 0.6 subtract_divide_fusion.2
  295.8 0.6 subtract_divide_fusion.2
  305.9 0.6 subtract_divide_fusion.2
  307.4 0.6 subtract_divide_fusion.2
  308.5 1.0 copy.44
  (883 shorter events, 120.9 us)
Async XLA Ops:
  3.2 24.6 %collective-permute-start.2 = (bf16[64,3,2,3,128]{4,0,3,2,1:T(8,128)(2,1)}, bf16[64,3,2,3,128]{4,0,3,2,1:T(8,128)(2,1)}, u32[]{:S(2)}, u32[]{:S(2)}) collective-permute-start(bf16[64,3,2,3,128]{4,0,3,2,1:T(8,128)(2,1)} %copy.39), channel_id=1, source_target_pairs={{0,2},{2,4},{4,6},{6,8},{8,10},{10,12},{12,14},{14,16},{16,18},{18... | collective-permute-start | bytes 884744 | tf_op jit(solution)/shard_map/ppermute | solution.py:15
  6.2 16.2 %copy-start = (bf16[64,3,8,8,128]{4,3,2,1,0:T(8,128)(2,1)S(1)}, bf16[64,3,8,8,128]{4,3,2,1,0:T(8,128)(2,1)}, u32[]{:S(2)}) copy-start(bf16[64,3,8,8,128]{4,3,2,1,0:T(8,128)(2,1)} %param.6) | copy-start | bytes 9437188
  11.6 13.7 %collective-permute-start = (bf16[64,3,2,8,3]{0,3,4,2,1:T(8,128)(2,1)}, bf16[64,3,2,8,3]{0,3,4,2,1:T(8,128)(2,1)}, u32[]{:S(2)}, u32[]{:S(2)}) collective-permute-start(bf16[64,3,2,8,3]{0,3,4,2,1:T(8,128)(2,1)} %copy.36), channel_id=1, source_target_pairs={{0,1},{2,3},{4,5},{6,7},{8,9},{10,11},{12,13},{14,15},{16,17},{18,... | collective-permute-start | bytes 55304 | tf_op jit(solution)/shard_map/ppermute | solution.py:15
  16.0 10.5 %collective-permute-start.1 = (bf16[64,3,2,8,3]{0,3,4,2,1:T(8,128)(2,1)}, bf16[64,3,2,8,3]{0,3,4,2,1:T(8,128)(2,1)}, u32[]{:S(2)}, u32[]{:S(2)}) collective-permute-start(bf16[64,3,2,8,3]{0,3,4,2,1:T(8,128)(2,1)} %copy.38), channel_id=1, source_target_pairs={{1,0},{3,2},{5,4},{7,6},{9,8},{11,10},{13,12},{15,14},{17,16},{19,... | collective-permute-start | bytes 55304 | tf_op jit(solution)/shard_map/ppermute | solution.py:18
  18.1 11.3 %collective-permute-start.3 = (bf16[64,3,2,3,128]{4,0,3,2,1:T(8,128)(2,1)}, bf16[64,3,2,3,128]{4,0,3,2,1:T(8,128)(2,1)S(1)}, u32[]{:S(2)}, u32[]{:S(2)}) collective-permute-start(bf16[64,3,2,3,128]{4,0,3,2,1:T(8,128)(2,1)} %copy.40), channel_id=1, source_target_pairs={{2,0},{4,2},{6,4},{8,6},{10,8},{12,10},{14,12},{16,14},{18,16},{20... | collective-permute-start | bytes 884744 | tf_op jit(solution)/shard_map/ppermute | solution.py:18
  22.6 2.7 copy-start.3
  25.3 3.5 %slice-start = ((bf16[64,3,8,8,128]{4,3,2,1,0:T(8,128)(2,1)}), bf16[64,3,2,8,128]{4,3,2,1,0:T(8,128)(2,1)S(1)}, s32[]{:S(2)}) async-start(bf16[64,3,8,8,128]{4,3,2,1,0:T(8,128)(2,1)} %param.6), calls=%async_computation | async-start | bytes 1572864 | tf_op jit(solution)/shard_map/slice | solution.py:68
  30.1 1.2 copy-start.1
  31.4 1.2 copy-start.2
